TPU v7x, 32 devices: a whole 2x2x4 slice. The times are simulated.
32 devices in a mesh: dp: 16 (over z, y, x), aug: 2 (over core).
Axes of the slice: x: 2, y: 2, z: 4, core: 2. Of those that a mesh axis runs over, the one named last changes fastest.
Arguments:
- images: bfloat16 [2, 16, 197, 768], P('aug', 'dp'), may hold values from -6 to 6
- out_grads: bfloat16 [2, 16, 197, 768], P('aug', 'dp'), may hold values from -8 to 8
- up_weight_t: bfloat16 [3072, 768], P(('dp', 'aug')), may hold values from -0.21875 to 0.21875
- down_weight_t: bfloat16 [3072, 768], P(('dp', 'aug')), may hold values from -0.21875 to 0.21875
- left_up: bfloat16 [3072, 128], P(('dp', 'aug')), may hold values from -0.109375 to 0.109375
- right_up: bfloat16 [768, 128], replicated, may hold values from -0.21875 to 0.21875
- left_down: bfloat16 [768, 128], replicated, may hold values from -0.21875 to 0.21875
- right_down: bfloat16 [3072, 128], P(('dp', 'aug')), may hold values from -0.109375 to 0.109375
- noise: float32 [2, 128, 128], P(None, 'aug'), may hold values from -6 to 6
Outputs:
- update: float32 [2, 128, 128], P(None, 'aug')
- clip_scales: float32 [16], P('dp')
All inputs are finite; a program needn't handle non-finite values.
Results may differ from a plain program's by a relative error of at most 0.0032.
Values may be sent and summed in bfloat16 or wider, within the bound.
A program may use at most 64 MiB of HBM per device.

v0:
```python
import math
import jax
import jax.numpy as jnp
from jax import lax
from jax.sharding import PartitionSpec as P

gelu_coef = 0.7978845608028654
clip_frac = 0.3
noise_mult = 0.05


def gelu_pair(hidden):
    inner = gelu_coef * (hidden + 0.044715 * hidden * hidden * hidden)
    tangent = jnp.tanh(inner)
    value = 0.5 * hidden * (1.0 + tangent)
    slope = 0.5 * (1.0 + tangent) + 0.5 * hidden * (1.0 - tangent * tangent) * gelu_coef * (
        1.0 + 3.0 * 0.044715 * hidden * hidden
    )
    return (value, slope)


def contract_last(left, right):
    return lax.dot_general(
        left, right, (((1,), (1,)), ((), ())), preferred_element_type=jnp.float32
    )


def local(
    images, out_grads, up_weight_t, down_weight_t, left_up, right_up, left_down, right_down, noise
):
    local_augs = images.shape[0]
    local_images = images.shape[1]
    tokens = images.shape[2]
    width = images.shape[3]
    rank = right_up.shape[1]
    token_rows = images.reshape(-1, width)
    grad_rows = out_grads.reshape(-1, width)
    up_piece = lax.all_gather(up_weight_t, ("dp", "aug"), axis=0, tiled=True)
    down_piece = lax.all_gather(down_weight_t, ("dp", "aug"), axis=0, tiled=True)
    left_piece = lax.all_gather(left_up, ("dp", "aug"), axis=0, tiled=True)
    right_piece = lax.all_gather(right_down, ("dp", "aug"), axis=0, tiled=True)
    hidden = contract_last(token_rows, up_piece)
    activation, slope = gelu_pair(hidden)
    back = contract_last(grad_rows, down_piece)
    hidden_grad = (back * slope).astype(jnp.bfloat16)
    first = jnp.dot(hidden_grad, left_piece, preferred_element_type=jnp.float32)
    second = jnp.dot(
        activation.astype(jnp.bfloat16), right_piece, preferred_element_type=jnp.float32
    )
    up_total = first
    down_total = second
    v_up = up_total.astype(jnp.bfloat16)
    u_down = down_total.astype(jnp.bfloat16)
    u_up = jnp.dot(token_rows, right_up, preferred_element_type=jnp.float32).astype(jnp.bfloat16)
    v_down = jnp.dot(grad_rows, left_down, preferred_element_type=jnp.float32).astype(jnp.bfloat16)
    shape = (local_augs, local_images, tokens, rank)
    first = jnp.einsum(
        "aitr,aits->irs",
        v_up.reshape(shape),
        u_up.reshape(shape),
        preferred_element_type=jnp.float32,
    )
    second = jnp.einsum(
        "aitr,aits->irs",
        v_down.reshape(shape),
        u_down.reshape(shape),
        preferred_element_type=jnp.float32,
    )
    local_terms = jnp.stack([first, second], axis=1)
    all_augs = local_augs * lax.axis_size("aug")
    row_sums = lax.psum_scatter(local_terms, "aug", scatter_dimension=2, tiled=True)
    my_rows = row_sums / all_augs
    squares = lax.psum(jnp.sum(my_rows * my_rows, axis=(1, 2, 3)), "aug")
    norms = jnp.sqrt(squares + 1e-06)
    clip_norm = clip_frac * rank * math.sqrt(tokens / all_augs)
    clip_scales = jnp.minimum(1.0, clip_norm / norms)
    clipped_rows = jnp.sum(clip_scales[:, None, None, None] * my_rows, axis=0)
    summed_rows = lax.psum(clipped_rows, "dp")
    all_images = local_images * lax.axis_size("dp")
    update = (summed_rows + noise_mult * clip_norm * noise) / jnp.sqrt(jnp.float32(all_images))
    return (update, clip_scales)


def solution(mesh):
    placed = (
        P("aug", "dp", None, None),
        P("aug", "dp", None, None),
        P(("dp", "aug"), None),
        P(("dp", "aug"), None),
        P(("dp", "aug"), None),
        P(),
        P(),
        P(("dp", "aug"), None),
        P(None, "aug", None),
    )
    return jax.shard_map(
        local,
        mesh=mesh,
        in_specs=placed,
        out_specs=(P(None, "aug", None), P("dp")),
        check_vma=False,
    )
```

profile of v0, /device:TPU:0, one launch (start us, length us, event | category | flops | bytes accessed | tf_op | source)
XLA Modules:
  0.0 281.8 jit_solution(15459410550856716134)
XLA Ops:
  7.2 0.0 copy-start
  7.2 0.0 all-gather.5.cloned.1.call-start
  7.2 0.7 all-gather.5.cloned.1.call-update
  7.9 0.0 all-gather.3.cloned.1.call-start
  8.0 0.7 all-gather.3.cloned.1.call-update
  8.7 0.0 reduce-scatter.2.cloned.1.call-start
  8.7 46.2 %all_gather.14 = bf16[3072,128]{1,0:T(8,128)(2,1)S(1)} all-gather(bf16[96,128]{1,0:T(8,128)(2,1)} %param.13), channel_id=1, replica_groups=mesh['dp'=16,'aug'=2] {'dp','aug'}, dimensions={0}, use_global_device_ids=true | all-gather | bytes 811008 | tf_op jit(solution)/shard_map/all_gather | solution.py:40
  54.9 42.6 %all_gather.15 = bf16[3072,128]{1,0:T(8,128)(2,1)} all-gather(bf16[96,128]{1,0:T(8,128)(2,1)} %param.16), channel_id=1, replica_groups=mesh['dp'=16,'aug'=2] {'dp','aug'}, dimensions={0}, use_global_device_ids=true | all-gather | bytes 811008 | tf_op jit(solution)/shard_map/all_gather | solution.py:41
  97.5 0.0 all-gather.5.cloned.1.call-done
  97.5 0.0 copy-done
  97.5 0.0 copy-start.1
  97.5 4.0 %fusion.17 = f32[197,3072]{1,0:T(8,128)S(1)} fusion(bf16[3072,768]{1,0:T(8,128)(2,1)} %all-gather.5.cloned.1.call-done, bf16[1,1,197,768]{3,2,1,0:T(8,128)(2,1)S(1)} %copy-done), kind=kOutput, calls=%fused_computation.24 | convolution fusion | flops 929562624 | bytes 7441920 | tf_op jit(solution)/shard_map/dot_general | solution.py:23
  101.5 0.0 copy-done.1
  101.5 1.6 fusion.14
  103.1 42.8 %all-gather.3.cloned.1.call-done = bf16[3072,768]{1,0:T(8,128)(2,1)} async-done(((bf16[96,768]{1,0:T(8,128)(2,1)}), bf16[3072,768]{1,0:T(8,128)(2,1)}) %all-gather.3.cloned.1.call-update) | async-done | bytes 4718608 | tf_op jit(solution)/shard_map/all_gather | solution.py:39
  145.9 5.6 %fusion.13 = bf16[197,128]{1,0:T(8,128)(2,1)} fusion(bf16[3072,128]{1,0:T(8,128)(2,1)S(1)} %all_gather.14, bf16[3072,768]{1,0:T(8,128)(2,1)} %all-gather.3.cloned.1.call-done, f32[197,3072]{1,0:T(8,128)S(1)} %fusion.17, bf16[1,1,197,768]{3,2,1,0:T(8,128)(2,1)} %param.10), kind=kOutput, calls=%fused_computation.17 | convolution fusion | flops 1096013440 | bytes 8278784 | tf_op jit(solution)/shard_map/dot_general | solution.py:46
  151.5 1.4 convolution_bitcast_fusion.1
  152.9 1.5 convolution_bitcast_fusion
  154.4 0.7 pad_maximum_fusion
  155.1 0.0 reduce-scatter.2.cloned.1.call-update
  155.1 0.0 all-reduce.2.cloned.1.call-start
  155.1 6.0 %reduce-scatter.2.cloned.1.call-done = f32[1,2,64,128]{3,2,1,0:T(8,128)} async-done(((f32[1,2,128,128]{3,2,1,0:T(8,128)}), f32[1,2,64,128]{3,2,1,0:T(8,128)}) %reduce-scatter.2.cloned.1.call-update) | async-done | bytes 65552 | tf_op jit(solution)/shard_map/reduce_scatter | solution.py:71
  161.1 1.5 multiply_reduce_fusion
  162.6 3.1 %psum.14 = f32[1]{0:T(128)} all-reduce(f32[1]{0:T(128)} %bitcast.4), channel_id=1, replica_groups=mesh['dp'=16,'aug'=2] {'aug'}, use_global_device_ids=true, to_apply=%region_2.0 | all-reduce | flops 1 | bytes 8 | tf_op jit(solution)/shard_map/psum | solution.py:73
  166.4 1.5 multiply_bitcast_fusion
  167.8 0.0 all-reduce.2.cloned.1.call-update
  167.9 104.8 %all-reduce.2.cloned.1.call-done = f32[2,64,128]{2,1,0:T(8,128)} async-done(((f32[2,64,128]{2,1,0:T(8,128)}), f32[2,64,128]{2,1,0:T(8,128)}) %all-reduce.2.cloned.1.call-update) | async-done | bytes 65552 | tf_op jit(solution)/shard_map/psum | solution.py:78
  272.6 1.5 add_multiply_fusion
Async XLA Ops:
  7.2 90.3 %copy-start = (bf16[1,1,197,768]{3,2,1,0:T(8,128)(2,1)S(1)}, bf16[1,1,197,768]{3,2,1,0:T(8,128)(2,1)}, u32[]{:S(2)}) copy-start(bf16[1,1,197,768]{3,2,1,0:T(8,128)(2,1)} %param.9) | copy-start | bytes 907780
  7.2 90.3 %all-gather.5.cloned.1.call-start = ((), (), s32[]{:S(2)}) async-start(), calls=%async_computation.2 | async-start | bytes 4866048 | tf_op jit(solution)/shard_map/all_gather | solution.py:38
  7.9 138.0 %all-gather.3.cloned.1.call-start = ((), (), s32[]{:S(2)}) async-start(), calls=%async_computation.1 | async-start | bytes 4866048 | tf_op jit(solution)/shard_map/all_gather | solution.py:39
  8.7 152.5 %reduce-scatter.2.cloned.1.call-start = ((), (), s32[]{:S(2)}) async-start(), calls=%async_computation.3 | async-start | bytes 196608 | tf_op jit(solution)/shard_map/reduce_scatter | solution.py:71
  97.5 4.0 %copy-start.1 = (bf16[3072,128]{1,0:T(8,128)(2,1)S(1)}, bf16[3072,128]{1,0:T(8,128)(2,1)}, u32[]{:S(2)}) copy-start(bf16[3072,128]{1,0:T(8,128)(2,1)} %all_gather.15) | copy-start | bytes 2359300
  155.1 117.5 %all-reduce.2.cloned.1.call-start = ((), (), s32[]{:S(2)}) async-start(), calls=%async_computation.4 | async-start | bytes 131072 | tf_op jit(solution)/shard_map/psum | solution.py:78
Sparse Core Ops, SparseCore 0:
  10.9 69.5 all-gather.4
  83.4 62.4 all-gather.2
  155.2 5.8 reduce-scatter.1
  168.0 104.5 all-reduce.1
where the time goes:
time: 282 us
  waiting for transfers between devices  155 us (55%)
  blocking collectives  91.9 us (33%)
  between operations  15.6 us (6%)
  matrix products  14.1 us (5%)
  other arithmetic  5.11 us (2%)
    psum x1, waiting for transfers between devices, local(): summed_rows = lax.psum(clipped_rows, 'dp')  105 us
    all_gather x1, blocking collectives, local(): left_piece = lax.all_gather(left_up, ('dp', 'aug'), axis=0, tiled=True)  46.2 us
    all_gather x1, waiting for transfers between devices, local(): lax.all_gather(down_weight_t, ('dp', 'aug'), axis=0, tiled=True)  42.8 us
    all_gather x1, blocking collectives, local(): right_piece = lax.all_gather(right_down, ('dp', 'aug'), axis=0, tiled=True)  42.6 us
    reduce_scatter x1, waiting for transfers between devices, local(): lax.psum_scatter(local_terms, 'aug', scatter_dimension=2, tiled=True)  5.99 us
  transfers between devices with their start and end apart: 4, of which 3 were waited for; matrix products, arithmetic and copies ran while one was open for 2% of the time, Pallas kernels for 0%

commit v1 on v0

--- a/solution.py
+++ b/solution.py
@@ -75,7 +75,8 @@
     clip_norm = clip_frac * rank * math.sqrt(tokens / all_augs)
     clip_scales = jnp.minimum(1.0, clip_norm / norms)
     clipped_rows = jnp.sum(clip_scales[:, None, None, None] * my_rows, axis=0)
-    summed_rows = lax.psum(clipped_rows, "dp")
+    parts = lax.all_gather(clipped_rows, "dp", axis=0, tiled=False)
+    summed_rows = parts.sum(axis=0)
     all_images = local_images * lax.axis_size("dp")
     update = (summed_rows + noise_mult * clip_norm * noise) / jnp.sqrt(jnp.float32(all_images))
     return (update, clip_scales)

time: 282 us -> 234 us (0.83)
  waiting for transfers between devices: 155 us -> 107 us
    psum x1 -> x0, waiting for transfers between devices: 105 us -> none  [local(): summed_rows = lax.psum(clipped_rows, 'dp')]
    all_gather x0 -> x1, waiting for transfers between devices: none -> 56.4 us  [local(): parts = lax.all_gather(clipped_rows, 'dp', axis=0, tiled=False)]
where the time goes in v1:
time: 234 us
  waiting for transfers between devices  107 us (46%)
  blocking collectives  91.9 us (39%)
  between operations  15.6 us (7%)
  matrix products  14.2 us (6%)
  other arithmetic  5.53 us (2%)
    all_gather x1, waiting for transfers between devices, local(): parts = lax.all_gather(clipped_rows, 'dp', axis=0, tiled=False)  56.4 us
    all_gather x1, blocking collectives, local(): left_piece = lax.all_gather(left_up, ('dp', 'aug'), axis=0, tiled=True)  46.2 us
    all_gather x1, waiting for transfers between devices, local(): lax.all_gather(down_weight_t, ('dp', 'aug'), axis=0, tiled=True)  42.8 us
    all_gather x1, blocking collectives, local(): right_piece = lax.all_gather(right_down, ('dp', 'aug'), axis=0, tiled=True)  42.6 us
    reduce_scatter x1, waiting for transfers between devices, local(): lax.psum_scatter(local_terms, 'aug', scatter_dimension=2, tiled=True)  5.99 us
    dot_general x1, matrix products, local(): first = jnp.dot(hidden_grad, left_piece, preferred_element_type=jnp.float32)  5.61 us
  transfers between devices with their start and end apart: 4, of which 3 were waited for; matrix products, arithmetic and copies ran while one was open for 2% of the time, Pallas kernels for 0%

profile of v1, /device:TPU:0, one launch (start us, length us, event | category | flops | bytes accessed | tf_op | source)
XLA Modules:
  0.0 233.9 jit_solution(16129593150368034898)
XLA Ops:
  7.2 0.0 copy-start
  7.2 0.0 all-gather.6.cloned.1.call-start
  7.2 0.7 all-gather.6.cloned.1.call-update
  7.9 0.0 all-gather.4.cloned.1.call-start
  8.0 0.7 all-gather.4.cloned.1.call-update
  8.7 0.0 reduce-scatter.2.cloned.1.call-start
  8.7 46.2 %all_gather.18 = bf16[3072,128]{1,0:T(8,128)(2,1)S(1)} all-gather(bf16[96,128]{1,0:T(8,128)(2,1)} %param.13), channel_id=1, replica_groups=mesh['dp'=16,'aug'=2] {'dp','aug'}, dimensions={0}, use_global_device_ids=true | all-gather | bytes 811008 | tf_op jit(solution)/shard_map/all_gather | solution.py:40
  54.9 42.6 %all_gather.19 = bf16[3072,128]{1,0:T(8,128)(2,1)} all-gather(bf16[96,128]{1,0:T(8,128)(2,1)} %param.16), channel_id=1, replica_groups=mesh['dp'=16,'aug'=2] {'dp','aug'}, dimensions={0}, use_global_device_ids=true | all-gather | bytes 811008 | tf_op jit(solution)/shard_map/all_gather | solution.py:41
  97.5 0.0 all-gather.6.cloned.1.call-done
  97.5 0.0 copy-done
  97.5 0.0 copy-start.1
  97.5 4.0 %fusion.17 = f32[197,3072]{1,0:T(8,128)S(1)} fusion(bf16[3072,768]{1,0:T(8,128)(2,1)} %all-gather.6.cloned.1.call-done, bf16[1,1,197,768]{3,2,1,0:T(8,128)(2,1)S(1)} %copy-done), kind=kOutput, calls=%fused_computation.24 | convolution fusion | flops 929562624 | bytes 7441920 | tf_op jit(solution)/shard_map/dot_general | solution.py:23
  101.5 0.0 copy-done.1
  101.5 1.6 fusion.14
  103.1 42.8 %all-gather.4.cloned.1.call-done = bf16[3072,768]{1,0:T(8,128)(2,1)} async-done(((bf16[96,768]{1,0:T(8,128)(2,1)}), bf16[3072,768]{1,0:T(8,128)(2,1)}) %all-gather.4.cloned.1.call-update) | async-done | bytes 4718608 | tf_op jit(solution)/shard_map/all_gather | solution.py:39
  145.9 5.6 %fusion.13 = bf16[197,128]{1,0:T(8,128)(2,1)} fusion(bf16[3072,128]{1,0:T(8,128)(2,1)S(1)} %all_gather.18, bf16[3072,768]{1,0:T(8,128)(2,1)} %all-gather.4.cloned.1.call-done, f32[197,3072]{1,0:T(8,128)S(1)} %fusion.17, bf16[1,1,197,768]{3,2,1,0:T(8,128)(2,1)} %param.10), kind=kOutput, calls=%fused_computation.17 | convolution fusion | flops 1096013440 | bytes 8278784 | tf_op jit(solution)/shard_map/dot_general | solution.py:46
  151.5 0.0 copy-start.2
  151.5 1.4 convolution_bitcast_fusion.1
  152.9 1.5 convolution_bitcast_fusion
  154.4 0.7 pad_maximum_fusion
  155.1 0.0 reduce-scatter.2.cloned.1.call-update
  155.1 0.0 all-gather.8.cloned.1.call-start
  155.2 6.0 %reduce-scatter.2.cloned.1.call-done = f32[1,2,64,128]{3,2,1,0:T(8,128)} async-done(((f32[1,2,128,128]{3,2,1,0:T(8,128)}), f32[1,2,64,128]{3,2,1,0:T(8,128)}) %reduce-scatter.2.cloned.1.call-update) | async-done | bytes 65552 | tf_op jit(solution)/shard_map/reduce_scatter | solution.py:71
  161.2 1.5 multiply_reduce_fusion
  162.6 3.1 %psum.7 = f32[1]{0:T(128)} all-reduce(f32[1]{0:T(128)} %bitcast.4), channel_id=1, replica_groups=mesh['dp'=16,'aug'=2] {'aug'}, use_global_device_ids=true, to_apply=%region_2.0 | all-reduce | flops 1 | bytes 8 | tf_op jit(solution)/shard_map/psum | solution.py:73
  166.4 1.5 broadcast_multiply_fusion
  167.9 0.0 all-gather.8.cloned.1.call-update
  167.9 56.4 %all-gather.8.cloned.1.call-done = f32[16,2,64,128]{3,2,1,0:T(8,128)} async-done(((f32[1,2,64,128]{3,2,1,0:T(8,128)}), f32[16,2,64,128]{3,2,1,0:T(8,128)}) %all-gather.8.cloned.1.call-update) | async-done | bytes 1048592 | tf_op jit(solution)/shard_map/all_gather | solution.py:78
  224.3 1.3 reduce_sum.26
  225.6 0.0 copy-done.2
  225.6 0.6 add_multiply_fusion
Async XLA Ops:
  7.2 90.3 %copy-start = (bf16[1,1,197,768]{3,2,1,0:T(8,128)(2,1)S(1)}, bf16[1,1,197,768]{3,2,1,0:T(8,128)(2,1)}, u32[]{:S(2)}) copy-start(bf16[1,1,197,768]{3,2,1,0:T(8,128)(2,1)} %param.9) | copy-start | bytes 907780
  7.2 90.3 %all-gather.6.cloned.1.call-start = ((), (), s32[]{:S(2)}) async-start(), calls=%async_computation.2 | async-start | bytes 4866048 | tf_op jit(solution)/shard_map/all_gather | solution.py:38
  7.9 138.0 %all-gather.4.cloned.1.call-start = ((), (), s32[]{:S(2)}) async-start(), calls=%async_computation.1 | async-start | bytes 4866048 | tf_op jit(solution)/shard_map/all_gather | solution.py:39
  8.7 152.5 %reduce-scatter.2.cloned.1.call-start = ((), (), s32[]{:S(2)}) async-start(), calls=%async_computation.3 | async-start | bytes 196608 | tf_op jit(solution)/shard_map/reduce_scatter | solution.py:71
  97.5 4.0 %copy-start.1 = (bf16[3072,128]{1,0:T(8,128)(2,1)S(1)}, bf16[3072,128]{1,0:T(8,128)(2,1)}, u32[]{:S(2)}) copy-start(bf16[3072,128]{1,0:T(8,128)(2,1)} %all_gather.19) | copy-start | bytes 2359300
  151.5 74.1 %copy-start.2 = (f32[2,64,128]{2,1,0:T(8,128)S(1)}, f32[2,64,128]{2,1,0:T(8,128)}, u32[]{:S(2)}) copy-start(f32[2,64,128]{2,1,0:T(8,128)} %param.17) | copy-start | bytes 196612
  155.1 69.1 %all-gather.8.cloned.1.call-start = ((), (), s32[]{:S(2)}) async-start(), calls=%async_computation.4 | async-start | bytes 1114112 | tf_op jit(solution)/shard_map/all_gather | solution.py:78
Sparse Core Ops, SparseCore 0:
  10.9 69.5 all-gather.5
  83.4 62.4 all-gather.3
  155.3 5.8 reduce-scatter.1
  168.0 56.2 all-gather.7
